TPU v7x, 256 devices: a whole 4x4x8 slice. The times are simulated.
256 devices in a mesh: tm: 32 (over y, z), eval: 8 (over x, core).
Axes of the slice: x: 4, y: 4, z: 8, core: 2. Of those that a mesh axis runs over, the one named last changes fastest.
Arguments:
- hidden: bfloat16 [512, 1024, 1536], P('tm', 'eval'), may hold values from -9 to 9
- modulation: float32 [512, 2, 1536], P('tm'), may hold values from -2 to 3
- head_weight: bfloat16 [64, 1536], replicated, may hold values from -1 to 1
- real_score: bfloat16 [64, 21, 16, 4096], P('eval', None, None, 'tm'), may hold values from -152917 to 152917
- fake_score: bfloat16 [64, 21, 16, 4096], P('eval', None, None, 'tm'), may hold values from -152917 to 152917
- window_start: int32 [64], P('eval'), may hold values from 0 to 491, as said below
- timestep: int32 [64], P('eval'), may hold values from 20 to 999
Outputs:
- d_hidden: bfloat16 [512, 1024, 1536], P('tm', 'eval')
- head_grad: float32 [64, 1536], replicated
- mod_grad: float32 [512, 2, 1536], P('tm')
Inputs may be any that keep to these rules, and one draw needn't show every extreme that they name: `window_start`: every window lies inside the rollout; one window starts at frame 0 and one at the last possible frame.
All inputs are finite; a program needn't handle non-finite values.
Results may differ from a plain program's by a relative error of at most 0.0012.
The roundings to bfloat16 on the way count: a program that leaves them out, or rounds other values in their place, can miss the bound.
Values may be sent and summed in bfloat16 or wider, within the bound.
No kernel may reach another device: no remote copies, remote signals or barrier semaphores. Data moves between devices by JAX's collectives and lax.ppermute only.
A program may use at most 128 MiB of HBM per device.

v0:
```python
import jax
import jax.numpy as jnp
from jax import lax
from jax.sharding import PartitionSpec as P

C = 16
PATCH = 4
WIN = 21
TOK = 1024


def layer_norm(values_in):
    values = values_in.astype(jnp.float32)
    center = jnp.mean(values, axis=-1, keepdims=True)
    shifted = values - center
    inv_std = lax.rsqrt(jnp.mean(shifted * shifted, axis=-1, keepdims=True) + 1e-06)
    return (shifted * inv_std, inv_std)


def per_device(hidden, modulation, head_weight, real_score, fake_score, window_start, timestep):
    frames_dev, tok_dev, width = hidden.shape
    shift = modulation[:, 0][:, None, :]
    scale = modulation[:, 1][:, None, :]
    normed, inv_std = layer_norm(hidden)
    adapted = (normed * (1.0 + scale) + shift).astype(jnp.bfloat16)
    head_out = jnp.einsum("ftd,od->fto", adapted, head_weight, preferred_element_type=jnp.float32)
    latent = head_out.astype(jnp.bfloat16).reshape(frames_dev, tok_dev, C, PATCH)
    latent = latent.transpose(0, 2, 1, 3).reshape(frames_dev, C, tok_dev * PATCH)
    frame_whole = lax.all_gather(latent, "eval", axis=2, tiled=True)
    latent_all = lax.all_to_all(frame_whole, "tm", split_axis=2, concat_axis=0, tiled=True)
    pixel_block = latent_all.shape[2]
    frame_index = window_start[:, None] + jnp.arange(WIN, dtype=jnp.int32)[None, :]
    window_latent = latent_all[frame_index].astype(jnp.float32)
    real_values = real_score.astype(jnp.float32)
    fake_values = fake_score.astype(jnp.float32)
    abs_sums = jnp.sum(jnp.abs(window_latent - real_values), axis=(1, 2, 3))
    totals = lax.psum(abs_sums, "tm")
    normalizer = totals / (WIN * C * PATCH * TOK) + 1e-05
    weight = timestep.astype(jnp.float32) / 1000.0 / normalizer
    window_grad = weight[:, None, None, None] * (fake_values - real_values)
    group_grad = (
        jnp.zeros(latent_all.shape, jnp.float32)
        .at[frame_index.reshape(-1)]
        .add(window_grad.reshape(-1, C, pixel_block))
    )
    home = lax.all_to_all(group_grad, "tm", split_axis=0, concat_axis=2, tiled=True)
    owner_grad = lax.psum_scatter(home, "eval", scatter_dimension=2, tiled=True)
    upstream = owner_grad.reshape(frames_dev, C, tok_dev, PATCH).transpose(0, 2, 1, 3)
    upstream = upstream.reshape(frames_dev, tok_dev, C * PATCH).astype(jnp.bfloat16)
    d_adapted = jnp.einsum("fto,od->ftd", upstream, head_weight, preferred_element_type=jnp.float32)
    head_part = jnp.einsum("fto,ftd->od", upstream, adapted, preferred_element_type=jnp.float32)
    mod_part = jnp.stack([jnp.sum(d_adapted, axis=1), jnp.sum(d_adapted * normed, axis=1)], axis=1)
    head_grad = lax.psum(head_part, ("tm", "eval"))
    mod_grad = lax.psum(mod_part, "eval")
    d_normed = d_adapted * (1.0 + scale)
    d_hidden = inv_std * (
        d_normed
        - jnp.mean(d_normed, axis=-1, keepdims=True)
        - normed * jnp.mean(d_normed * normed, axis=-1, keepdims=True)
    )
    return (d_hidden.astype(jnp.bfloat16), head_grad, mod_grad)


def solution(mesh):
    placed = (
        P("tm", "eval", None),
        P("tm", None, None),
        P(),
        P("eval", None, None, "tm"),
        P("eval", None, None, "tm"),
        P("eval"),
        P("eval"),
    )
    return jax.shard_map(
        per_device,
        mesh=mesh,
        in_specs=placed,
        out_specs=(P("tm", "eval", None), P(), P("tm", None, None)),
        check_vma=False,
    )
```

profile of v0, /device:TPU:1, one launch (start us, length us, event | category | flops | bytes accessed | tf_op | source)
XLA Modules:
  0.0 757.5 jit_solution(7772980234880290092)
XLA Ops:
  7.2 3.8 convert_reduce_fusion
  11.1 4.6 fusion.13
  15.9 3.1 fusion.24
  19.0 3.2 copy.49
  22.2 2.3 copy.50
  24.5 32.2 %all-gather.2.cloned.1.call-done = bf16[16,16,4096]{2,1,0:T(8,128)(2,1)} async-done(((bf16[16,16,512]{2,1,0:T(8,128)(2,1)}), bf16[16,16,4096]{2,1,0:T(8,128)(2,1)}) %all-gather.2.cloned.1.call-update) | async-done | bytes 2097168 | tf_op jit(solution)/shard_map/all_gather | solution.py:29
  56.7 15.4 %copy.51 = bf16[16,16,4096]{1,0,2:T(8,128)(2,1)} copy(bf16[16,16,4096]{2,1,0:T(8,128)(2,1)} %all-gather.2.cloned.1.call-done) | data formatting | bytes 4194304 | tf_op jit(solution)/shard_map/all_gather | solution.py:29
  72.0 20.8 %reshape.132 = bf16[32,2,16384]{2,1,0:T(2,128)(2,1)} reshape(bf16[4096,16,16]{2,1,0:T(8,128)(2,1)} %bitcast.43) | data formatting | bytes 4194304
  92.8 9.6 %all-to-all-start = ((bf16[32,2,16384]{2,1,0:T(2,128)(2,1)}), bf16[32,2,16384]{2,1,0:T(2,128)(2,1)S(1)}, u32[]{:S(2)}, u32[]{:S(2)}) async-start(bf16[32,2,16384]{2,1,0:T(2,128)(2,1)} %reshape.132), calls=%async_computation | async-start | bytes 4194304 | tf_op jit(solution)/shard_map/all_to_all | solution.py:30
  102.8 48.5 %all-to-all-done = bf16[32,2,16384]{2,1,0:T(2,128)(2,1)S(1)} async-done(((bf16[32,2,16384]{2,1,0:T(2,128)(2,1)}), bf16[32,2,16384]{2,1,0:T(2,128)(2,1)S(1)}, u32[]{:S(2)}, u32[]{:S(2)}) %all-to-all-start) | async-done | bytes 2097184 | tf_op jit(solution)/shard_map/all_to_all | solution.py:30
  151.3 14.4 %reshape.133 = bf16[4096,16,16]{2,1,0:T(8,128)(2,1)} reshape(bf16[32,2,16384]{2,1,0:T(2,128)(2,1)S(1)} %all-to-all-done) | data formatting | bytes 4194304
  165.7 14.4 %copy.53 = bf16[32,16,16,128]{3,2,1,0:T(8,128)(2,1)S(1)} copy(bf16[32,16,16,128]{2,1,3,0:T(8,128)(2,1)} %bitcast.44) | data formatting | bytes 4194304 | tf_op jit(solution)/shard_map/all_to_all | solution.py:30
  180.1 1.6 gather_fusion
  181.7 1.4 fusion.22
  183.1 60.2 %psum.21 = f32[8]{0:T(128)S(1)} all-reduce(f32[8]{0:T(128)S(1)} %fusion.22), channel_id=1, replica_groups=mesh['tm'=32,'eval'=8] {'tm'}, use_global_device_ids=true, to_apply=%region_3.0 | all-reduce | flops 8 | bytes 64 | tf_op jit(solution)/shard_map/psum | solution.py:37
  243.4 1.3 fusion.23
  244.7 2.3 broadcast_in_dim.2
  247.0 19.7 %scatter_fusion = f32[512,16,128]{2,1,0:T(8,128)} fusion(f32[512,16,128]{2,1,0:T(8,128)} %broadcast_in_dim.2, s32[168]{0:T(256)S(1)} %bitcast.59, f32[168,16,128]{2,1,0:T(8,128)S(1)} %bitcast.51), kind=kCustom, calls=%fused_computation.1 | custom fusion | flops 344064 | bytes 4129440 | tf_op jit(solution)/shard_map/scatter-add | solution.py:44
  266.7 83.4 %all_to_all.36 = f32[512,16,128]{2,1,0:T(8,128)S(1)} all-to-all(f32[512,16,128]{2,1,0:T(8,128)} %scatter_fusion), channel_id=1, replica_groups=mesh['tm'=32,'eval'=8] {'tm'}, dimensions={0} | all-to-all | bytes 8388608 | tf_op jit(solution)/shard_map/all_to_all | solution.py:46
  350.1 2.5 copy.76
  352.7 50.7 %reduce-scatter.2.cloned.1.call-done = f32[16,16,512]{2,1,0:T(8,128)} async-done(((f32[16,16,4096]{2,1,0:T(8,128)}), f32[16,16,512]{2,1,0:T(8,128)}) %reduce-scatter.2.cloned.1.call-update) | async-done | bytes 524304 | tf_op jit(solution)/shard_map/reduce_scatter | solution.py:47
  403.4 1.1 convert_element_type.43
  404.5 2.8 copy.55
  407.3 4.0 copy.56
  411.3 10.1 %fusion.12 = (f32[16,1536]{1,0:T(8,128)S(1)}, f32[16,128]{1,0:T(8,128)S(1)}, f32[16,128]{1,0:T(8,128)S(1)}, f32[16,1536]{1,0:T(8,128)S(1)}, f32[16,128,1536]{2,1,0:T(8,128)}) fusion(bf16[16,128,1536]{2,1,0:T(8,128)(2,1)} %param.7, f32[16,128]{1,0:T(8,128)S(1)} %add_rsqrt_fusion, f32[16,128]{1,0:T(8,128)S(1)} %broadcast_multiply_fusion.2, ...), kind=kOutput, calls=%fused_computation.16 | convolution fusion | flops 434057216 | bytes 19660800 | tf_op jit(solution)/shard_map/fto,od->ftd/dot_general | solution.py:50
  421.4 3.5 fusion.18
  424.9 0.7 pad_maximum_fusion
  426.2 10.5 %fusion.11 = bf16[16,128,1536]{2,1,0:T(8,128)(2,1)} fusion(bf16[16,128,1536]{2,1,0:T(8,128)(2,1)} %param.7, f32[16,128,1536]{2,1,0:T(8,128)} %get-tuple-element.24, f32[16,128]{1,0:T(8,128)S(1)} %broadcast_multiply_fusion, f32[16,128]{1,0:T(8,128)S(1)} %broadcast_multiply_fusion.1, f32[16,1536]{1,0:T(8,128)S(1)} %get-tuple-element.26, ...), kind=kLoop, calls=%fused_computation.15 | loop fusion | flops 28311552 | bytes 25296896 | tf_op jit(solution)/shard_map/convert_element_type | solution.py:61
  436.7 53.9 %all-reduce.5.cloned.1.call-done = f32[16,2,1536]{2,0,1:T(8,128)} async-done(((f32[16,2,1536]{2,0,1:T(8,128)}), f32[16,2,1536]{2,0,1:T(8,128)}) %all-reduce.5.cloned.1.call-update) | async-done | bytes 196624 | tf_op jit(solution)/shard_map/psum | solution.py:54
  490.5 1.8 copy.59
  492.3 256.9 %all-reduce.3.cloned.1.call-done = f32[64,1536]{1,0:T(8,128)} async-done(((f32[64,1536]{1,0:T(8,128)}), f32[64,1536]{1,0:T(8,128)}) %all-reduce.3.cloned.1.call-update) | async-done | bytes 393232 | tf_op jit(solution)/shard_map/psum | solution.py:53
  749.2 1.8 copy.80
  (38 shorter events, 1.3 us)
Async XLA Ops:
  7.2 8.7 %copy-start = (bf16[64,1536]{1,0:T(8,128)(2,1)S(1)}, bf16[64,1536]{1,0:T(8,128)(2,1)}, u32[]{:S(2)}) copy-start(bf16[64,1536]{1,0:T(8,128)(2,1)} %param.9) | copy-start | bytes 589828
  7.2 8.5 %copy-start.3 = (f32[16,2,1536]{2,1,0:T(2,128)S(1)}, f32[16,2,1536]{2,1,0:T(2,128)}, u32[]{:S(2)}) copy-start(f32[16,2,1536]{2,1,0:T(2,128)} %param.8) | copy-start | bytes 589828
  7.2 49.5 %all-gather.2.cloned.1.call-start = ((), (), s32[]{:S(2)}) async-start(), calls=%async_computation.3 | async-start | bytes 2359296 | tf_op jit(solution)/shard_map/all_gather | solution.py:29
  7.2 8.7 %copy-start.1 = (bf16[16,128,1536]{2,1,0:T(8,128)(2,1)S(1)}, bf16[16,128,1536]{2,1,0:T(8,128)(2,1)}, u32[]{:S(2)}) copy-start(bf16[16,128,1536]{2,1,0:T(8,128)(2,1)} %param.7) | copy-start | bytes 18874372
  72.0 30.4 %copy-start.4 = (s32[8]{0:T(128)S(1)}, s32[8]{0:T(128)}, u32[]{:S(2)}) copy-start(s32[8]{0:T(128)} %param.12) | copy-start | bytes 100
  92.8 58.5 %all-to-all-start = ((bf16[32,2,16384]{2,1,0:T(2,128)(2,1)}), bf16[32,2,16384]{2,1,0:T(2,128)(2,1)S(1)}, u32[]{:S(2)}, u32[]{:S(2)}) async-start(bf16[32,2,16384]{2,1,0:T(2,128)(2,1)} %reshape.132), calls=%async_computation | async-start | bytes 4194304 | tf_op jit(solution)/shard_map/all_to_all | solution.py:30
  102.4 301.0 %reduce-scatter.2.cloned.1.call-start = ((), (), s32[]{:S(2)}) async-start(), calls=%async_computation.4 | async-start | bytes 4718592 | tf_op jit(solution)/shard_map/reduce_scatter | solution.py:47
  165.7 16.0 %copy-start.2 = (bf16[8,21,16,128]{3,2,1,0:T(8,128)(2,1)S(1)}, bf16[8,21,16,128]{3,2,1,0:T(8,128)(2,1)}, u32[]{:S(2)}) copy-start(bf16[8,21,16,128]{3,2,1,0:T(8,128)(2,1)} %param.10) | copy-start | bytes 2064388
  165.7 77.7 %copy-start.5 = (s32[8]{0:T(128)S(1)}, s32[8]{0:T(128)}, u32[]{:S(2)}) copy-start(s32[8]{0:T(128)} %param.13) | copy-start | bytes 100
  352.7 137.9 %all-reduce.5.cloned.1.call-start = ((), (), s32[]{:S(2)}) async-start(), calls=%async_computation.6 | async-start | bytes 393216 | tf_op jit(solution)/shard_map/psum | solution.py:54
  407.3 14.2 %slice-start = ((s8[6291456]{0:T(1024)(128)(4,1)}), s8[2097152]{0:T(1024)(128)(4,1)S(1)}, s32[]{:S(2)}) async-start(s8[6291456]{0:T(1024)(128)(4,1)} %bitcast.45), calls=%async_computation.7 | async-start | bytes 4194304
  411.3 10.1 %slice-start.1 = ((s8[6291456]{0:T(1024)(128)(4,1)}), s8[4194304]{0:T(1024)(128)(4,1)S(1)}, s32[]{:S(2)}) async-start(s8[6291456]{0:T(1024)(128)(4,1)} %bitcast.45), calls=%async_computation.8 | async-start | bytes 8388608
  425.6 323.6 %all-reduce.3.cloned.1.call-start = ((), (), s32[]{:S(2)}) async-start(), calls=%async_computation.5 | async-start | bytes 786432 | tf_op jit(solution)/shard_map/psum | solution.py:53
Sparse Core Ops, SparseCore 0:
  24.6 31.9 all-gather.1
  352.8 50.5 reduce-scatter.1
  425.7 64.7 all-reduce.4
  496.5 252.6 all-reduce.2
where the time goes:
time: 760 us; the launch traced here: 758 us
  waiting for transfers between devices  443 us (58%)
  blocking collectives  144 us (19%)
  local copies, waits for them, and re-layouts  87.5 us (12%)
  other arithmetic  43.3 us (6%)
  matrix products  16.6 us (2%)
  between operations  14 us (2%)
  starting transfers between devices  9.73 us (1%)
    psum x1, waiting for transfers between devices, per_device(): head_grad = lax.psum(head_part, ('tm', 'eval'))  257 us
    all_to_all x1, blocking collectives, per_device(): lax.all_to_all(group_grad, 'tm', split_axis=0, concat_axis=2, tiled=True)  83.4 us
    psum x1, blocking collectives, per_device(): totals = lax.psum(abs_sums, 'tm')  60.2 us
    psum x1, waiting for transfers between devices, per_device(): mod_grad = lax.psum(mod_part, 'eval')  53.9 us
    reduce_scatter x1, waiting for transfers between devices, per_device(): owner_grad = lax.psum_scatter(home, 'eval', scatter_dimension=2, tiled=True)  50.7 us
    all_to_all x1, waiting for transfers between devices, per_device(): lax.all_to_all(frame_whole, 'tm', split_axis=2, concat_axis=0, tiled=True)  48.5 us
    unnamed x20, local copies, waits for them, and re-layouts  38.7 us
    all_gather x1, waiting for transfers between devices, per_device(): frame_whole = lax.all_gather(latent, 'eval', axis=2, tiled=True)  32.2 us
  transfers between devices with their start and end apart: 5, of which 5 were waited for; matrix products, arithmetic and copies ran while one was open for 2% of the time, Pallas kernels for 0%

commit v1 on v0

--- a/solution.py
+++ b/solution.py
@@ -50,7 +50,7 @@
     d_adapted = jnp.einsum("fto,od->ftd", upstream, head_weight, preferred_element_type=jnp.float32)
     head_part = jnp.einsum("fto,ftd->od", upstream, adapted, preferred_element_type=jnp.float32)
     mod_part = jnp.stack([jnp.sum(d_adapted, axis=1), jnp.sum(d_adapted * normed, axis=1)], axis=1)
-    head_grad = lax.psum(head_part, ("tm", "eval"))
+    head_grad = lax.psum(lax.psum(head_part, "eval"), "tm")
     mod_grad = lax.psum(mod_part, "eval")
     d_normed = d_adapted * (1.0 + scale)
     d_hidden = inv_std * (

time: 760 us -> 653 us (0.86)
  waiting for transfers between devices: 443 us -> 333 us
    psum x2, waiting for transfers between devices: 311 us -> 202 us  [per_device(): head_grad = lax.psum(lax.psum(head_part, 'eval'), 'tm')]
    unnamed x20 -> x22, local copies, waits for them, and re-layouts: 38.7 us -> 37.8 us
where the time goes in v1:
time: 653 us; the launch traced here: 647 us
  waiting for transfers between devices  333 us (51%)
  blocking collectives  144 us (22%)
  local copies, waits for them, and re-layouts  86.6 us (13%)
  other arithmetic  43.3 us (7%)
  matrix products  16.6 us (3%)
  between operations  14 us (2%)
  starting transfers between devices  9.73 us (1%)
    psum x2, waiting for transfers between devices, per_device(): head_grad = lax.psum(lax.psum(head_part, 'eval'), 'tm')  202 us
    all_to_all x1, blocking collectives, per_device(): lax.all_to_all(group_grad, 'tm', split_axis=0, concat_axis=2, tiled=True)  83.4 us
    psum x1, blocking collectives, per_device(): totals = lax.psum(abs_sums, 'tm')  60.2 us
    reduce_scatter x1, waiting for transfers between devices, per_device(): owner_grad = lax.psum_scatter(home, 'eval', scatter_dimension=2, tiled=True)  50.7 us
    all_to_all x1, waiting for transfers between devices, per_device(): lax.all_to_all(frame_whole, 'tm', split_axis=2, concat_axis=0, tiled=True)  48.5 us
    unnamed x22, local copies, waits for them, and re-layouts  37.8 us
    all_gather x1, waiting for transfers between devices, per_device(): frame_whole = lax.all_gather(latent, 'eval', axis=2, tiled=True)  32.2 us
    scatter-add x1, other arithmetic, per_device(): group_grad = jnp.zeros(latent_all.shape, jnp.float32).at[frame_index.resh...  19.7 us
  transfers between devices with their start and end apart: 5, of which 5 were waited for; matrix products, arithmetic and copies ran while one was open for 2% of the time, Pallas kernels for 0%

profile of v1, /device:TPU:1, one launch (start us, length us, event | category | flops | bytes accessed | tf_op | source)
XLA Modules:
  0.0 647.1 jit_solution(4845662212469694354)
XLA Ops:
  7.2 3.8 convert_reduce_fusion
  11.1 4.6 fusion.13
  15.9 3.1 fusion.24
  19.0 3.2 copy.49
  22.2 2.3 copy.50
  24.5 32.2 %all-gather.2.cloned.1.call-done = bf16[16,16,4096]{2,1,0:T(8,128)(2,1)} async-done(((bf16[16,16,512]{2,1,0:T(8,128)(2,1)}), bf16[16,16,4096]{2,1,0:T(8,128)(2,1)}) %all-gather.2.cloned.1.call-update) | async-done | bytes 2097168 | tf_op jit(solution)/shard_map/all_gather | solution.py:29
  56.7 15.4 %copy.51 = bf16[16,16,4096]{1,0,2:T(8,128)(2,1)} copy(bf16[16,16,4096]{2,1,0:T(8,128)(2,1)} %all-gather.2.cloned.1.call-done) | data formatting | bytes 4194304 | tf_op jit(solution)/shard_map/all_gather | solution.py:29
  72.0 20.8 %reshape.132 = bf16[32,2,16384]{2,1,0:T(2,128)(2,1)} reshape(bf16[4096,16,16]{2,1,0:T(8,128)(2,1)} %bitcast.43) | data formatting | bytes 4194304
  92.8 9.6 %all-to-all-start = ((bf16[32,2,16384]{2,1,0:T(2,128)(2,1)}), bf16[32,2,16384]{2,1,0:T(2,128)(2,1)S(1)}, u32[]{:S(2)}, u32[]{:S(2)}) async-start(bf16[32,2,16384]{2,1,0:T(2,128)(2,1)} %reshape.132), calls=%async_computation | async-start | bytes 4194304 | tf_op jit(solution)/shard_map/all_to_all | solution.py:30
  102.8 48.5 %all-to-all-done = bf16[32,2,16384]{2,1,0:T(2,128)(2,1)S(1)} async-done(((bf16[32,2,16384]{2,1,0:T(2,128)(2,1)}), bf16[32,2,16384]{2,1,0:T(2,128)(2,1)S(1)}, u32[]{:S(2)}, u32[]{:S(2)}) %all-to-all-start) | async-done | bytes 2097184 | tf_op jit(solution)/shard_map/all_to_all | solution.py:30
  151.3 14.4 %reshape.133 = bf16[4096,16,16]{2,1,0:T(8,128)(2,1)} reshape(bf16[32,2,16384]{2,1,0:T(2,128)(2,1)S(1)} %all-to-all-done) | data formatting | bytes 4194304
  165.7 14.4 %copy.53 = bf16[32,16,16,128]{3,2,1,0:T(8,128)(2,1)S(1)} copy(bf16[32,16,16,128]{2,1,3,0:T(8,128)(2,1)} %bitcast.44) | data formatting | bytes 4194304 | tf_op jit(solution)/shard_map/all_to_all | solution.py:30
  180.1 1.6 gather_fusion
  181.7 1.4 fusion.22
  183.1 60.2 %psum.28 = f32[8]{0:T(128)S(1)} all-reduce(f32[8]{0:T(128)S(1)} %fusion.22), channel_id=1, replica_groups=mesh['tm'=32,'eval'=8] {'tm'}, use_global_device_ids=true, to_apply=%region_3.0 | all-reduce | flops 8 | bytes 64 | tf_op jit(solution)/shard_map/psum | solution.py:37
  243.4 1.3 fusion.23
  244.7 2.3 broadcast_in_dim.2
  247.0 19.7 %scatter_fusion = f32[512,16,128]{2,1,0:T(8,128)} fusion(f32[512,16,128]{2,1,0:T(8,128)} %broadcast_in_dim.2, s32[168]{0:T(256)S(1)} %bitcast.59, f32[168,16,128]{2,1,0:T(8,128)S(1)} %bitcast.51), kind=kCustom, calls=%fused_computation.1 | custom fusion | flops 344064 | bytes 4129440 | tf_op jit(solution)/shard_map/scatter-add | solution.py:44
  266.7 83.4 %all_to_all.36 = f32[512,16,128]{2,1,0:T(8,128)S(1)} all-to-all(f32[512,16,128]{2,1,0:T(8,128)} %scatter_fusion), channel_id=1, replica_groups=mesh['tm'=32,'eval'=8] {'tm'}, dimensions={0} | all-to-all | bytes 8388608 | tf_op jit(solution)/shard_map/all_to_all | solution.py:46
  350.1 2.5 copy.76
  352.7 50.7 %reduce-scatter.2.cloned.1.call-done = f32[16,16,512]{2,1,0:T(8,128)} async-done(((f32[16,16,4096]{2,1,0:T(8,128)}), f32[16,16,512]{2,1,0:T(8,128)}) %reduce-scatter.2.cloned.1.call-update) | async-done | bytes 524304 | tf_op jit(solution)/shard_map/reduce_scatter | solution.py:47
  403.4 1.1 convert_element_type.43
  404.5 2.8 copy.55
  407.3 4.0 copy.56
  411.3 10.1 %fusion.12 = (f32[16,1536]{1,0:T(8,128)S(1)}, f32[16,128]{1,0:T(8,128)S(1)}, f32[16,128]{1,0:T(8,128)S(1)}, f32[16,1536]{1,0:T(8,128)S(1)}, f32[16,128,1536]{2,1,0:T(8,128)}) fusion(bf16[16,128,1536]{2,1,0:T(8,128)(2,1)} %param.7, f32[16,128]{1,0:T(8,128)S(1)} %add_rsqrt_fusion, f32[16,128]{1,0:T(8,128)S(1)} %broadcast_multiply_fusion.2, ...), kind=kOutput, calls=%fused_computation.16 | convolution fusion | flops 434057216 | bytes 19660800 | tf_op jit(solution)/shard_map/fto,od->ftd/dot_general | solution.py:50
  421.4 3.5 fusion.18
  424.9 0.7 pad_maximum_fusion
  425.7 66.1 %all-reduce.6.cloned.1.call-done = (f32[64,1536]{1,0:T(8,128)}, f32[16,2,1536]{2,0,1:T(8,128)}) async-done(((f32[64,1536]{1,0:T(8,128)}, f32[16,2,1536]{2,0,1:T(8,128)}), (f32[64,1536]{1,0:T(8,128)}, f32[16,2,1536]{2,0,1:T(8,128)})) %all-reduce.6.cloned.1.call-update) | async-done | bytes 589840 | tf_op jit(solution)/shard_map/psum | solution.py:53
  491.8 10.5 %fusion.11 = bf16[16,128,1536]{2,1,0:T(8,128)(2,1)} fusion(bf16[16,128,1536]{2,1,0:T(8,128)(2,1)} %param.7, f32[16,128,1536]{2,1,0:T(8,128)} %get-tuple-element.26, f32[16,128]{1,0:T(8,128)S(1)} %broadcast_multiply_fusion, f32[16,128]{1,0:T(8,128)S(1)} %broadcast_multiply_fusion.1, f32[16,1536]{1,0:T(8,128)S(1)} %get-tuple-element.28, ...), kind=kLoop, calls=%fused_computation.15 | loop fusion | flops 28311552 | bytes 25296896 | tf_op jit(solution)/shard_map/convert_element_type | solution.py:61
  502.3 0.8 copy.59
  503.2 135.7 %all-reduce.4.cloned.1.call-done = f32[64,1536]{1,0:T(8,128)} async-done(((f32[64,1536]{1,0:T(8,128)}), f32[64,1536]{1,0:T(8,128)}) %all-reduce.4.cloned.1.call-update) | async-done | bytes 393232 | tf_op jit(solution)/shard_map/psum | solution.py:53
  638.8 1.8 copy.81
  (40 shorter events, 0.8 us)
Async XLA Ops:
  7.2 8.7 %copy-start = (bf16[64,1536]{1,0:T(8,128)(2,1)S(1)}, bf16[64,1536]{1,0:T(8,128)(2,1)}, u32[]{:S(2)}) copy-start(bf16[64,1536]{1,0:T(8,128)(2,1)} %param.9) | copy-start | bytes 589828
  7.2 8.5 %copy-start.3 = (f32[16,2,1536]{2,1,0:T(2,128)S(1)}, f32[16,2,1536]{2,1,0:T(2,128)}, u32[]{:S(2)}) copy-start(f32[16,2,1536]{2,1,0:T(2,128)} %param.8) | copy-start | bytes 589828
  7.2 49.5 %all-gather.2.cloned.1.call-start = ((), (), s32[]{:S(2)}) async-start(), calls=%async_computation.3 | async-start | bytes 2359296 | tf_op jit(solution)/shard_map/all_gather | solution.py:29
  7.2 8.7 %copy-start.1 = (bf16[16,128,1536]{2,1,0:T(8,128)(2,1)S(1)}, bf16[16,128,1536]{2,1,0:T(8,128)(2,1)}, u32[]{:S(2)}) copy-start(bf16[16,128,1536]{2,1,0:T(8,128)(2,1)} %param.7) | copy-start | bytes 18874372
  72.0 30.4 %copy-start.5 = (s32[8]{0:T(128)S(1)}, s32[8]{0:T(128)}, u32[]{:S(2)}) copy-start(s32[8]{0:T(128)} %param.12) | copy-start | bytes 100
  92.8 58.5 %all-to-all-start = ((bf16[32,2,16384]{2,1,0:T(2,128)(2,1)}), bf16[32,2,16384]{2,1,0:T(2,128)(2,1)S(1)}, u32[]{:S(2)}, u32[]{:S(2)}) async-start(bf16[32,2,16384]{2,1,0:T(2,128)(2,1)} %reshape.132), calls=%async_computation | async-start | bytes 4194304 | tf_op jit(solution)/shard_map/all_to_all | solution.py:30
  102.4 301.0 %reduce-scatter.2.cloned.1.call-start = ((), (), s32[]{:S(2)}) async-start(), calls=%async_computation.4 | async-start | bytes 4718592 | tf_op jit(solution)/shard_map/reduce_scatter | solution.py:47
  165.7 16.0 %copy-start.2 = (bf16[8,21,16,128]{3,2,1,0:T(8,128)(2,1)S(1)}, bf16[8,21,16,128]{3,2,1,0:T(8,128)(2,1)}, u32[]{:S(2)}) copy-start(bf16[8,21,16,128]{3,2,1,0:T(8,128)(2,1)} %param.10) | copy-start | bytes 2064388
  165.7 77.7 %copy-start.6 = (s32[8]{0:T(128)S(1)}, s32[8]{0:T(128)}, u32[]{:S(2)}) copy-start(s32[8]{0:T(128)} %param.13) | copy-start | bytes 100
  352.7 139.1 %all-reduce.6.cloned.1.call-start = ((), (), s32[]{:S(2)}) async-start(), calls=%async_computation.6 | async-start | bytes 1179648 | tf_op jit(solution)/shard_map/psum | solution.py:53
  407.3 14.2 %slice-start = ((s8[6291456]{0:T(1024)(128)(4,1)}), s8[2097152]{0:T(1024)(128)(4,1)S(1)}, s32[]{:S(2)}) async-start(s8[6291456]{0:T(1024)(128)(4,1)} %bitcast.45), calls=%async_computation.7 | async-start | bytes 4194304
  411.3 10.1 %slice-start.1 = ((s8[6291456]{0:T(1024)(128)(4,1)}), s8[4194304]{0:T(1024)(128)(4,1)S(1)}, s32[]{:S(2)}) async-start(s8[6291456]{0:T(1024)(128)(4,1)} %bitcast.45), calls=%async_computation.8 | async-start | bytes 8388608
  425.6 213.2 %all-reduce.4.cloned.1.call-start = ((), (), s32[]{:S(2)}) async-start(), calls=%async_computation.5 | async-start | bytes 786432 | tf_op jit(solution)/shard_map/psum | solution.py:53
  491.8 10.5 %copy-start.4 = (f32[16,2,1536]{2,0,1:T(8,128)S(1)}, f32[16,2,1536]{2,0,1:T(8,128)}, u32[]{:S(2)}) copy-start(f32[16,2,1536]{2,0,1:T(8,128)} %get-tuple-element.23) | copy-start | bytes 589828
Sparse Core Ops, SparseCore 0:
  24.6 31.9 all-gather.1
  352.8 50.5 reduce-scatter.1
  425.7 66.0 all-reduce.5
  495.1 143.7 all-reduce.3
